TPU v7x, 32 devices: a whole 2x2x4 slice. The times are simulated.
32 devices in a mesh: slab: 8 (over z, y), rep: 4 (over x, core).
Axes of the slice: x: 2, y: 2, z: 4, core: 2. Of those that a mesh axis runs over, the one named last changes fastest.
Arguments:
- feats: bfloat16 [32768, 128], P(('slab', 'rep')), may hold values from -6 to 6
- cotangent: bfloat16 [32768, 128], P(('slab', 'rep')), may hold values from -6 to 6
- tile_table: bfloat16 [2048, 128, 128], P(('slab', 'rep')), as said below
- edge_src: int32 [32, 256], P(('slab', 'rep')), may hold values from 0 to 31
- edge_tile: int32 [32, 256], P(('slab', 'rep')), may hold values from 0 to 63
- edge_slot: int32 [32, 256], P(('slab', 'rep')), may hold values from 0 to 63
- edge_count: int32 [32], P(('slab', 'rep')), may hold values from 32 to 256, as said below
- slot_block: int32 [8, 64], replicated, may hold values from 0 to 31
- norm_gain: float32 [256], replicated, may hold values from 0.1 to 1.9
- w_in: bfloat16 [256, 512], replicated, may hold values from -0.375 to 0.375
- b_in: float32 [512], replicated, may hold values from -3 to 3
- w_out: bfloat16 [512, 128], replicated, may hold values from -0.25 to 0.25
Outputs:
- updated: bfloat16 [32768, 128], P(('slab', 'rep'))
- grad_feats: float32 [32768, 128], P(('slab', 'rep'))
- grad_gain: float32 [256], replicated
- grad_w_in: float32 [256, 512], replicated
- grad_b_in: float32 [512], replicated
- grad_w_out: float32 [512, 128], replicated
Inputs may be any that keep to these rules, and one draw needn't show every extreme that they name: `edge_count`: some device uses all 256 entries and some only 32. `tile_table`: entries are zero or a positive edge weight.
All inputs are finite; a program needn't handle non-finite values.
Results may differ from a plain program's by a relative error of at most 0.0061.
Values may be sent and summed in bfloat16 or wider, within the bound.
A program may use at most 64 MiB of HBM per device.

v0:
```python
import functools

import jax
import jax.numpy as jnp
from jax import lax
from jax.experimental import pallas as pl
from jax.experimental.pallas import tpu as pltpu
from jax.sharding import PartitionSpec as P

NEIGH = 8
SLOT_CAP = 8
MID = NEIGH // 2

RMS_EPS = 1e-06
EDGE_UNROLL = 8
AXES = ("slab", "rep")
VMEM = pl.BlockSpec(memory_space=pltpu.VMEM)
SMEM = pl.BlockSpec(memory_space=pltpu.SMEM)
DMA = pltpu.SemaphoreType.DMA


def remote(src, dst, send_sem, recv_sem, slab, rep):
    return pltpu.make_async_remote_copy(
        src_ref=src,
        dst_ref=dst,
        send_sem=send_sem,
        recv_sem=recv_sem,
        device_id=(slab, rep),
        device_id_type=pl.DeviceIdType.MESH,
    )


def greet(targets):
    barrier = pltpu.get_barrier_semaphore()
    for slab, rep in targets:
        pl.semaphore_signal(
            barrier, inc=1, device_id=(slab, rep), device_id_type=pl.DeviceIdType.MESH
        )
    pl.semaphore_wait(barrier, len(targets))


def place():
    slab, rep = lax.axis_index("slab"), lax.axis_index("rep")
    core = lax.rem(rep, 2)
    return slab, rep, core, lax.div(rep, 2), rep + 1 - 2 * core


def gather_rep(own, out, halves, pieces, send_sems, recv_sems, meanwhile):
    slab, rep, core, half, partner = place()
    rows = own.shape[0] // pieces

    def piece(ref, i):
        return ref.at[pl.ds(i * rows, rows)]

    far = []
    sems = 0
    for d in range(1, halves):
        peer = lax.rem(half + d, halves) * 2 + core
        for i in range(pieces):
            copy = remote(
                piece(own, i), piece(out.at[rep], i), send_sems.at[sems], recv_sems.at[sems], slab, peer
            )
            copy.start()
            far.append((copy, lax.rem(half + halves - d, halves) * 2 + core, i))
            sems += 1
    near = remote(own, out.at[rep], send_sems.at[sems], recv_sems.at[sems], slab, partner)
    near.start()
    sems += 1
    out[rep] = own[...]
    meanwhile()
    passed = [near]
    for copy, origin, i in far:
        copy.wait_recv()
        onward = remote(
            piece(out.at[origin], i),
            piece(out.at[origin], i),
            send_sems.at[sems],
            recv_sems.at[sems],
            slab,
            partner,
        )
        onward.start()
        passed.append(onward)
        sems += 1
    for copy in passed:
        copy.wait_recv()
    return [copy for copy, _, _ in far] + passed


def gather_sems(halves, pieces):
    return 2 * (halves - 1) * pieces + 1


def rep_targets(halves):
    slab, rep, core, half, partner = place()
    return [(slab, partner)] + [
        (slab, lax.rem(half + d, halves) * 2 + core) for d in range(1, halves)
    ]


def gather_kernel(halves, pieces, own, table_hbm, out, turned, table, table_sem, send_sems, recv_sems):
    load = pltpu.make_async_copy(table_hbm, table, table_sem)
    load.start()
    greet(rep_targets(halves))

    def meanwhile():
        load.wait()

        @pl.loop(0, table.shape[0])
        def _(t):
            turned[t] = table[t].T

    for copy in gather_rep(own, out, halves, pieces, send_sems, recv_sems, meanwhile):
        copy.wait_send()


def edge_kernel(by_slot, n_out, count, srcs, tiles, slots, table, given, out, acc):
    live = count[0]
    last = srcs.shape[1] - 1
    acc[...] = jnp.zeros_like(acc)

    def turn(i, carry):
        work = []
        for u in range(EDGE_UNROLL):
            at = i * EDGE_UNROLL + u
            e = jnp.minimum(at, last)
            src, slot = srcs[0, e], slots[0, e]
            read, write = (slot, src) if by_slot else (src, slot)
            product = jnp.dot(table[tiles[0, e]], given[read], preferred_element_type=jnp.float32)
            work.append((jnp.where(at < live, write, n_out), product))
        for write, product in work:
            acc[write] += product
        return carry

    lax.fori_loop(0, lax.div(live + EDGE_UNROLL - 1, EDGE_UNROLL), turn, 0)
    out[...] = acc[0:n_out].astype(out.dtype)


def edges(by_slot, n_out, count, srcs, tiles, slots, table, given):
    shape = (table.shape[1], given.shape[2])
    return pl.pallas_call(
        functools.partial(edge_kernel, by_slot, n_out),
        out_shape=jax.ShapeDtypeStruct((n_out, *shape), jnp.bfloat16),
        in_specs=[SMEM] * 4 + [VMEM] * 2,
        out_specs=VMEM,
        scratch_shapes=[pltpu.VMEM((n_out + 1, *shape), jnp.float32)],
    )(count, srcs, tiles, slots, table, given)


def slab_at(offset):
    n_slab = lax.axis_size("slab")
    return lax.rem(lax.axis_index("slab") + offset + n_slab, n_slab)


FAR_FIRST = sorted((g for g in range(NEIGH) if g != MID), key=lambda g: -abs(g - MID))
ORDER = FAR_FIRST + [MID]


def share(arrived, second, direct, crossing, far_s, far_r, on_s, on_r, straight_s, straight_r, halves, meanwhile):
    slab, rep, core, half, partner = place()
    order = [MID] + FAR_FIRST
    copies = []
    across = []
    for g in order:
        if g in second:
            second[g].wait_recv()
        own = arrived.at[g, core, half, pl.ds(0, crossing)]
        for d in range(1, halves):
            peer = lax.rem(half + d, halves) * 2 + core
            copy = remote(own, own, far_s.at[d - 1, g], far_r.at[d - 1, g], slab, peer)
            copy.start()
            across.append((g, d, copy))
        copy = remote(own, own, on_s.at[0, g], on_r.at[0, g], slab, partner)
        copy.start()
        copies.append(copy)
    meanwhile()
    for g, d, copy in across:
        copy.wait_recv()
        theirs = arrived.at[g, core, lax.rem(half + halves - d, halves), pl.ds(0, crossing)]
        onward = remote(theirs, theirs, on_s.at[d, g], on_r.at[d, g], slab, partner)
        onward.start()
        copies.append(onward)
    others = arrived.shape[3] - crossing
    if others:
        for g in order:
            for h in range(halves):
                if (g, h) in direct:
                    direct[g, h].wait_recv()
                here = arrived.at[g, core, h, pl.ds(crossing, others)]
                onward = remote(here, here, straight_s.at[h, g], straight_r.at[h, g], slab, partner)
                onward.start()
                copies.append(onward)
    for copy in copies:
        copy.wait_recv()
    sent = copies + [copy for _, _, copy in across] + list(second.values()) + list(direct.values())
    for copy in sent:
        copy.wait_send()


def spread_kernel(
    halves,
    part,
    arrived,
    from_core,
    to_far,
    from_far,
    outgoing,
    core_s,
    core_r,
    fold_s,
    fold_r,
    slab_s,
    slab_r,
    far_s,
    far_r,
    on_s,
    on_r,
):
    slab, rep, core, half, partner = place()
    greet(rep_targets(halves) + [(slab_at(MID - g), rep) for g in FAR_FIRST])
    f32 = jnp.float32
    first = {}
    for g in ORDER:
        first[g] = remote(
            part.at[g, 1 - core], from_core.at[g], core_s.at[g], core_r.at[g], slab, partner
        )
        first[g].start()
    cross = {}
    for g in ORDER:
        first[g].wait_recv()
        for d in range(1, halves):
            h = lax.rem(half + d, halves)
            total = part[g, core, h].astype(f32) + from_core[g, h].astype(f32)
            to_far[d - 1, g] = total.astype(jnp.bfloat16)
            cross[g, d] = remote(
                to_far.at[d - 1, g],
                from_far.at[d - 1, g],
                fold_s.at[d - 1, g],
                fold_r.at[d - 1, g],
                slab,
                h * 2 + core,
            )
            cross[g, d].start()
    second = {}
    for g in ORDER:
        total = part[g, core, half].astype(f32) + from_core[g, half].astype(f32)
        for d in range(1, halves):
            cross[g, d].wait_recv()
            total = total + from_far[d - 1, g].astype(f32)
        if g == MID:
            arrived[g, core, half] = total.astype(jnp.bfloat16)
        else:
            outgoing[g] = total.astype(jnp.bfloat16)
            second[g] = remote(
                outgoing.at[g],
                arrived.at[g, core, half],
                slab_s.at[g],
                slab_r.at[g],
                slab_at(g - MID),
                rep,
            )
            second[g].start()
    share(
        arrived,
        second,
        {},
        arrived.shape[3],
        far_s,
        far_r,
        on_s,
        on_r,
        None,
        None,
        halves,
        lambda: None,
    )
    for copy in list(first.values()) + list(cross.values()):
        copy.wait_send()


def node_kernel(
    slot_block,
    arrived,
    feats,
    cot,
    gain,
    w_in,
    b_in,
    w_out,
    updated,
    base,
    d_agg,
    packed,
    agg,
    g_in,
    g_out,
    g_gain,
    g_b,
):
    slab, rep = lax.axis_index("slab"), lax.axis_index("rep")
    f32, bf16 = jnp.float32, jnp.bfloat16
    own_blocks, block_rows, width = agg.shape
    n_slab = slot_block.shape[0]
    agg[...] = jnp.zeros_like(agg)

    @pl.loop(0, NEIGH * SLOT_CAP)
    def _(c):
        origin = lax.rem(slab - (lax.div(c, SLOT_CAP) - MID) + n_slab, n_slab)
        dest = slot_block[origin, c]

        @pl.when(lax.div(dest, own_blocks) == rep)
        def _():
            agg[lax.rem(dest, own_blocks)] += arrived[c].astype(f32)

    for ref in (g_in, g_out, g_gain, g_b):
        ref[...] = jnp.zeros_like(ref)
    step_blocks = 2 if own_blocks % 2 == 0 else 1
    rows = step_blocks * block_rows

    @pl.loop(0, own_blocks // step_blocks)
    def _(i):
        at = pl.ds(pl.multiple_of(i * rows, rows), rows)
        feat = feats[at].astype(f32)
        cots = cot[at]
        wide = jnp.concatenate(
            [feat, agg[pl.ds(i * step_blocks, step_blocks)].reshape(rows, width)], axis=1
        )
        inv = lax.rsqrt(jnp.mean(wide * wide, axis=1, keepdims=True) + RMS_EPS)
        scaled = wide * inv
        normed = (scaled * gain[...]).astype(bf16)
        pre = jnp.dot(normed, w_in[...], preferred_element_type=f32) + b_in[...]
        sg = jax.nn.sigmoid(pre)
        act = (pre * sg).astype(bf16)
        updated[at] = (feat + jnp.dot(act, w_out[...], preferred_element_type=f32)).astype(bf16)
        d_act = lax.dot_general(cots, w_out[...], (((1,), (1,)), ((), ())), preferred_element_type=f32)
        d_pre = d_act * sg * (1.0 + pre * (1.0 - sg))
        d_pre_b = d_pre.astype(bf16)
        d_normed = lax.dot_general(
            d_pre_b, w_in[...], (((1,), (1,)), ((), ())), preferred_element_type=f32
        )
        d_scaled = d_normed * gain[...]
        inner = jnp.mean(d_scaled * wide, axis=1, keepdims=True)
        d_wide = inv * d_scaled - inv * inv * inv * wide * inner
        base[at] = cots.astype(f32) + d_wide[:, :width]
        d_agg[at] = d_wide[:, width:].astype(bf16)
        g_in[...] += lax.dot_general(normed, d_pre_b, (((0,), (0,)), ((), ())), preferred_element_type=f32)
        g_out[...] += lax.dot_general(act, cots, (((0,), (0,)), ((), ())), preferred_element_type=f32)
        g_gain[...] += jnp.sum(d_normed * scaled, axis=0, keepdims=True)
        g_b[...] += jnp.sum(d_pre, axis=0, keepdims=True)

    packed[...] = jnp.zeros_like(packed)
    n = g_in.shape[0]
    for c in range(g_in.shape[1] // width):
        packed[n * c : n * (c + 1)] = g_in[:, width * c : width * (c + 1)].astype(bf16)
    n = n * (g_in.shape[1] // width)
    packed[n : n + g_out.shape[0]] = g_out[...].astype(bf16)
    n += g_out.shape[0]
    rest = [
        ref[:, width * c : width * (c + 1)]
        for ref in (g_gain, g_b)
        for c in range(ref.shape[1] // width)
    ]
    rest.append(jnp.zeros((16 - len(rest), width), f32))
    packed[n : n + 16] = jnp.concatenate(rest, axis=0).astype(bf16)


def return_kernel(
    halves,
    pieces,
    slot_block,
    own,
    grads,
    arrived,
    summed,
    gathered,
    outgoing,
    plain,
    w_core,
    w_to,
    w_far,
    w_rep,
    w_in,
    w_piece,
    gat_s,
    gat_r,
    slab_s,
    slab_r,
    far_s,
    far_r,
    on_s,
    on_r,
    plain_s,
    plain_r,
    straight_s,
    straight_r,
    wc_s,
    wc_r,
    wf_s,
    wf_r,
    ws_s,
    ws_r,
    wg_s,
    wg_r,
):
    slab, rep, core, half, partner = place()
    n_slab = slot_block.shape[0]
    peers = range(1, n_slab)
    greet(rep_targets(halves) + [(slab_at(d), rep) for d in peers])
    f32, bf16 = jnp.float32, jnp.bfloat16
    own_blocks = own.shape[0]
    per_rep = arrived.shape[3]
    crossing = outgoing.shape[1]
    sent = []
    w_cross = []

    def halves_of_weights():
        near = []
        for d in list(range(1, halves)) + [0]:
            h = lax.rem(half + d, halves)
            copy = remote(grads.at[h, 1 - core], w_core.at[h], wc_s.at[d], wc_r.at[d], slab, partner)
            copy.start()
            near.append((d, h, copy))
        for d, h, copy in near:
            copy.wait_recv()
            if d > 0:
                total = grads[h, core].astype(f32) + w_core[h].astype(f32)
                w_to[d - 1] = total.astype(bf16)
                cross = remote(
                    w_to.at[d - 1], w_far.at[d - 1], wf_s.at[d - 1], wf_r.at[d - 1], slab, h * 2 + core
                )
                cross.start()
                w_cross.append(cross)
            sent.append(copy)

    sent += gather_rep(own, gathered, halves, pieces, gat_s, gat_r, halves_of_weights)
    def pick(g, h, j):
        dest = slot_block[slab_at(MID - g), g * SLOT_CAP + (h + core * halves) * per_rep + j]
        return gathered[lax.div(dest, own_blocks), lax.rem(dest, own_blocks)]

    second = {}
    for g in ORDER:
        for j in range(crossing):
            if g == MID:
                arrived[g, core, half, j] = pick(g, half, j)
            else:
                outgoing[g, j] = pick(g, half, j)
        if g != MID:
            second[g] = remote(
                outgoing.at[g],
                arrived.at[g, core, half, pl.ds(0, crossing)],
                slab_s.at[g],
                slab_r.at[g],
                slab_at(MID - g),
                rep,
            )
            second[g].start()
    direct = {}
    for g in ORDER:
        for h in range(halves):
            for j in range(crossing, per_rep):
                if g == MID:
                    arrived[g, core, h, j] = pick(g, h, j)
                else:
                    plain[g, h, j - crossing] = pick(g, h, j)
            if g != MID and crossing < per_rep:
                direct[g, h] = remote(
                    plain.at[g, h],
                    arrived.at[g, core, h, pl.ds(crossing, per_rep - crossing)],
                    plain_s.at[h, g],
                    plain_r.at[h, g],
                    slab_at(MID - g),
                    rep,
                )
                direct[g, h].start()
    total = grads[half, core].astype(f32) + w_core[half].astype(f32)
    for d, copy in enumerate(w_cross):
        copy.wait_recv()
        total = total + w_far[d].astype(f32)
    w_rep[...] = total.astype(bf16)
    w_slab = []
    for d in peers:
        peer = slab_at(d)
        copy = remote(w_rep.at[peer], w_in.at[d - 1], ws_s.at[d - 1], ws_r.at[d - 1], peer, rep)
        copy.start()
        w_slab.append(copy)
    w_back = []

    def finish_weights():
        total = w_rep[slab].astype(f32)
        for d, copy in enumerate(w_slab):
            copy.wait_recv()
            total = total + w_in[d].astype(f32)
        w_piece[...] = total.astype(bf16)
        summed[slab] = total.astype(bf16)
        for d in peers:
            copy = remote(
                w_piece, summed.at[slab], wg_s.at[d - 1], wg_r.at[d - 1], slab_at(d), rep
            )
            copy.start()
            w_back.append(copy)

    share(
        arrived,
        second,
        direct,
        crossing,
        far_s,
        far_r,
        on_s,
        on_r,
        straight_s,
        straight_r,
        halves,
        finish_weights,
    )
    for copy in w_back:
        copy.wait_recv()
    for copy in sent + w_cross + w_slab + w_back:
        copy.wait_send()


def fold_kernel(
    halves, part, summed, out, grads, from_core, outgoing, from_far, core_s, core_r, far_s, far_r, gat_s, gat_r
):
    slab, rep, core, half, partner = place()
    f32 = jnp.float32
    greet(rep_targets(halves))
    near = []
    for d in list(range(1, halves)) + [0]:
        h = lax.rem(half + d, halves)
        copy = remote(part.at[h, 1 - core], from_core.at[h], core_s.at[d], core_r.at[d], slab, partner)
        copy.start()
        near.append((d, h, copy))
    far = []

    def fold():
        for d, h, copy in near:
            copy.wait_recv()
            total = part[h, core].astype(f32) + from_core[h].astype(f32)
            if d == 0:
                out[...] = total
            else:
                outgoing[d - 1] = total.astype(jnp.bfloat16)
                onward = remote(
                    outgoing.at[d - 1],
                    from_far.at[d - 1],
                    far_s.at[d - 1],
                    far_r.at[d - 1],
                    slab,
                    h * 2 + core,
                )
                onward.start()
                far.append(onward)

    sent = gather_rep(summed, grads, halves, 1, gat_s, gat_r, fold)
    for d, onward in enumerate(far):
        onward.wait_recv()
        out[...] += from_far[d].astype(f32)
    for copy in sent + far + [copy for _, _, copy in near]:
        copy.wait_send()


def final_kernel(scale, base, folded, grads, grad_feats, g_gain, g_in, g_b, g_out):
    grad_feats[...] = base[...] + folded[...]
    width = grads.shape[1]

    def part(at, n):
        return grads[at : at + n].astype(jnp.float32) * scale

    n, panels = g_in.shape[0], g_in.shape[1] // width
    for c in range(panels):
        g_in[:, width * c : width * (c + 1)] = part(n * c, n)
    n = n * panels
    g_out[...] = part(n, g_out.shape[0])
    rest = part(n + g_out.shape[0], 16)
    at = 0
    for ref in (g_gain, g_b):
        for c in range(ref.shape[1] // width):
            ref[:, width * c : width * (c + 1)] = rest[at : at + 1]
            at += 1


def comm(kernel, cid, out_shape, in_specs, scratch):
    return pl.pallas_call(
        kernel,
        out_shape=out_shape,
        in_specs=in_specs,
        out_specs=jax.tree.map(lambda _: VMEM, out_shape),
        scratch_shapes=scratch,
        compiler_params=pltpu.CompilerParams(collective_id=cid, has_side_effects=True),
    )


def body(
    feats,
    cotangent,
    tile_table,
    edge_src,
    edge_tile,
    edge_slot,
    edge_count,
    slot_block,
    norm_gain,
    w_in,
    b_in,
    w_out,
):
    n_slab = lax.axis_size("slab")
    n_rep = lax.axis_size("rep")
    halves = n_rep // 2
    rows_dev, width = feats.shape
    hidden = w_out.shape[0]
    block_rows = tile_table.shape[1]
    own_blocks = rows_dev // block_rows
    slab_blocks = own_blocks * n_rep
    slot_count = slot_block.shape[1]
    per_rep = SLOT_CAP // n_rep
    pieces = 4
    bf16, f32 = jnp.bfloat16, jnp.float32
    lists = (edge_count, edge_src, edge_tile, edge_slot)
    shape = jax.ShapeDtypeStruct

    def block(*lead):
        return pltpu.VMEM((*lead, block_rows, width), bf16)

    n_gat = gather_sems(halves, pieces)
    slab_feats, turned = comm(
        functools.partial(gather_kernel, halves, pieces),
        0,
        (
            shape((n_rep, own_blocks, block_rows, width), bf16),
            shape(tile_table.shape, bf16),
        ),
        [VMEM, pl.BlockSpec(memory_space=pl.ANY)],
        [pltpu.VMEM(tile_table.shape, bf16), DMA] + [DMA((n_gat,))] * 2,
    )(feats.reshape(own_blocks, block_rows, width), tile_table)
    slab_feats = slab_feats.reshape(slab_blocks, block_rows, width)
    partial_sums = edges(False, slot_count, *lists, tile_table, slab_feats)
    arrived_shape = (NEIGH, 2, halves, per_rep, block_rows, width)
    share_sems = [DMA((halves - 1, NEIGH))] * 2 + [DMA((halves, NEIGH))] * 2
    arrived = comm(
        functools.partial(spread_kernel, halves),
        1,
        shape(arrived_shape, bf16),
        [VMEM],
        [
            block(NEIGH, halves, per_rep),
            block(halves - 1, NEIGH, per_rep),
            block(halves - 1, NEIGH, per_rep),
            block(NEIGH, per_rep),
        ]
        + [DMA((NEIGH,))] * 2
        + [DMA((halves - 1, NEIGH))] * 2
        + [DMA((NEIGH,))] * 2
        + share_sems,
    )(partial_sums.reshape(arrived_shape))
    used = w_in.size // width + hidden + 16
    each = -(-used // (n_slab * n_rep * 16)) * 16
    updated, base, d_agg, packed = pl.pallas_call(
        node_kernel,
        out_shape=(
            shape((rows_dev, width), bf16),
            shape((rows_dev, width), f32),
            shape((rows_dev, width), bf16),
            shape((n_slab * n_rep * each, width), bf16),
        ),
        in_specs=[SMEM] + [VMEM] * 7,
        out_specs=(VMEM,) * 4,
        scratch_shapes=[
            pltpu.VMEM((own_blocks, block_rows, width), f32),
            pltpu.VMEM(w_in.shape, f32),
            pltpu.VMEM(w_out.shape, f32),
            pltpu.VMEM((1, 2 * width), f32),
            pltpu.VMEM((1, hidden), f32),
        ],
    )(
        slot_block,
        arrived.reshape(slot_count, block_rows, width),
        feats,
        cotangent,
        norm_gain.reshape(1, -1),
        w_in,
        b_in.reshape(1, -1),
        w_out,
    )
    weights = pltpu.VMEM((n_slab, each, width), bf16)
    many = pltpu.VMEM((halves - 1, n_slab, each, width), bf16)
    slot_grads, summed = comm(
        functools.partial(return_kernel, halves, pieces),
        2,
        (shape(arrived_shape, bf16), shape((n_slab, each, width), bf16)),
        [SMEM, VMEM, VMEM],
        [
            block(n_rep, own_blocks),
            block(NEIGH, per_rep - per_rep // 2),
            block(NEIGH, halves, max(per_rep // 2, 1)),
            pltpu.VMEM((halves, n_slab, each, width), bf16),
            many,
            many,
            weights,
            pltpu.VMEM((n_slab - 1, each, width), bf16),
            pltpu.VMEM((each, width), bf16),
        ]
        + [DMA((n_gat,))] * 2
        + [DMA((NEIGH,))] * 2
        + share_sems
        + [DMA((halves, NEIGH))] * 4
        + [DMA((halves,))] * 2
        + [DMA((halves - 1,))] * 2
        + [DMA((n_slab - 1,))] * 4,
    )(
        slot_block,
        d_agg.reshape(own_blocks, block_rows, width),
        packed.reshape(halves, 2, n_slab, each, width),
    )
    from_edges = edges(
        True, slab_blocks, *lists, turned, slot_grads.reshape(slot_count, block_rows, width)
    )
    n_sum = gather_sems(halves, 1)
    folded, grads = comm(
        functools.partial(fold_kernel, halves),
        3,
        (shape((rows_dev, width), f32), shape((n_rep, n_slab, each, width), bf16)),
        [VMEM, VMEM],
        [
            pltpu.VMEM((halves, rows_dev, width), bf16),
            pltpu.VMEM((halves - 1, rows_dev, width), bf16),
            pltpu.VMEM((halves - 1, rows_dev, width), bf16),
        ]
        + [DMA((halves,))] * 2
        + [DMA((halves - 1,))] * 2
        + [DMA((n_sum,))] * 2,
    )(from_edges.reshape(halves, 2, rows_dev, width), summed)
    scale = float(rows_dev * n_slab * n_rep) ** (-0.5)
    grad_feats, grad_gain, grad_w_in, grad_b_in, grad_w_out = pl.pallas_call(
        functools.partial(final_kernel, scale),
        out_shape=(
            shape((rows_dev, width), f32),
            shape((1, 2 * width), f32),
            shape(w_in.shape, f32),
            shape((1, hidden), f32),
            shape(w_out.shape, f32),
        ),
        in_specs=[VMEM] * 3,
        out_specs=(VMEM,) * 5,
    )(base, folded, grads.reshape(-1, width))
    return (
        updated,
        grad_feats,
        grad_gain.reshape(-1),
        grad_w_in,
        grad_b_in.reshape(-1),
        grad_w_out,
    )


def solution(mesh):
    placed = (
        P(("slab", "rep"), None),
        P(("slab", "rep"), None),
        P(("slab", "rep"), None, None),
        P(("slab", "rep"), None),
        P(("slab", "rep"), None),
        P(("slab", "rep"), None),
        P(("slab", "rep")),
        P(),
        P(),
        P(),
        P(),
        P(),
    )
    return jax.shard_map(
        body,
        mesh=mesh,
        in_specs=placed,
        out_specs=(P(("slab", "rep"), None), P(("slab", "rep"), None), P(), P(), P(), P()),
        check_vma=False,
    )
```

profile of v0, /device:TPU:0, one launch (start us, length us, event | category | flops | bytes accessed | tf_op | source)
XLA Modules:
  0.0 134.4 jit_solution(9989828347640677339)
XLA Ops:
  1.3 13.6 %shard_map.163 = (bf16[4,8,128,128]{3,2,1,0:T(8,128)(2,1)}, bf16[64,128,128]{2,1,0:T(8,128)(2,1)}) custom-call(bf16[8,128,128]{2,1,0:T(8,128)(2,1)} %bitcast.17, bf16[64,128,128]{2,1,0:T(8,128)(2,1)} %table.1), custom_call_target="tpu_custom_call" | custom-call | tf_op jit(solution)/shard_map/pallas_call | solution.py:627
  14.9 10.9 %shard_map.164 = bf16[64,128,128]{2,1,0:T(8,128)(2,1)} custom-call(s32[1]{0:T(128)S(6)} %copy.18.count, s32[1,256]{1,0:T(1,128)} %srcs.3, s32[1,256]{1,0:T(1,128)} %tiles.3, s32[1,256]{1,0:T(1,128)} %slots.3, bf16[64,128,128]{2,1,0:T(8,128)(2,1)} %table.1, bf16[32,128,128]{2,1,0:T(8,128)(2,1)} %bitcast.18), custom_call_target="tpu_custom_call" | custom-call | tf_op jit(solution)/shard_map/pallas_call | solution.py:141
  25.8 33.6 %shard_map.165 = bf16[8,2,2,2,128,128]{5,4,3,2,1,0:T(8,128)(2,1)} custom-call(bf16[8,2,2,2,128,128]{5,4,3,2,1,0:T(8,128)(2,1)} %bitcast.14), custom_call_target="tpu_custom_call" | custom-call | tf_op jit(solution)/shard_map/pallas_call | solution.py:641
  59.4 8.0 %shard_map.166 = (bf16[1024,128]{1,0:T(8,128)(2,1)}, f32[1024,128]{1,0:T(8,128)}, bf16[1024,128]{1,0:T(8,128)(2,1)}, bf16[2048,128]{1,0:T(8,128)(2,1)}) custom-call(s32[8,64]{1,0:T(8,128)} %slot_block.3, bf16[64,128,128]{2,1,0:T(8,128)(2,1)} %bitcast.13, bf16[1024,128]{1,0:T(8,128)(2,1)} %feats.1, bf16[1024,128]{1,0:T(8,128)(2,1)} %cot.1, ...), custom_call_target="tpu_custom_call" | custom-call | tf_op jit(solution)/shard_map/pallas_call | solution.py:659
  67.4 40.9 %shard_map.167 = (bf16[8,2,2,2,128,128]{5,4,3,2,1,0:T(8,128)(2,1)}, bf16[8,64,128]{2,1,0:T(8,128)(2,1)}) custom-call(s32[8,64]{1,0:T(8,128)} %slot_block.3, bf16[8,128,128]{2,1,0:T(8,128)(2,1)} %bitcast.21, bf16[2,2,8,64,128]{4,3,2,1,0:T(8,128)(2,1)} %bitcast.20), custom_call_target="tpu_custom_call" | custom-call | tf_op jit(solution)/shard_map/pallas_call | solution.py:688
  108.3 10.6 %shard_map.168 = bf16[32,128,128]{2,1,0:T(8,128)(2,1)} custom-call(s32[1]{0:T(128)S(6)} %copy.18.count, s32[1,256]{1,0:T(1,128)} %srcs.3, s32[1,256]{1,0:T(1,128)} %tiles.3, s32[1,256]{1,0:T(1,128)} %slots.3, bf16[64,128,128]{2,1,0:T(8,128)(2,1)} %get-tuple-element.24.table, bf16[64,128,128]{2,1,0:T(8,128)(2,1)} %bitcast.16), custom_call_target="tpu_custom_call" | custom-call | tf_op jit(solution)/shard_map/pallas_call | solution.py:141
  118.9 12.9 %shard_map.169 = (f32[1024,128]{1,0:T(8,128)}, bf16[4,8,64,128]{3,2,1,0:T(8,128)(2,1)}) custom-call(bf16[2,2,1024,128]{3,2,1,0:T(8,128)(2,1)} %bitcast.15, bf16[8,64,128]{2,1,0:T(8,128)(2,1)} %get-tuple-element.28.summed), custom_call_target="tpu_custom_call" | custom-call | tf_op jit(solution)/shard_map/pallas_call | solution.py:720
  131.9 2.5 %shard_map.170 = (f32[1024,128]{1,0:T(8,128)}, f32[1,256]{1,0:T(1,128)}, f32[256,512]{1,0:T(8,128)}, f32[1,512]{1,0:T(1,128)}, f32[512,128]{1,0:T(8,128)}) custom-call(f32[1024,128]{1,0:T(8,128)} %get-tuple-element.23.base, f32[1024,128]{1,0:T(8,128)} %get-tuple-element.29.folded, bf16[2048,128]{1,0:T(8,128)(2,1)} %bitcast.19), custom_call_target="tpu_custom_call" | custom-call | tf_op jit(solution)/shard_map/pallas_call | solution.py:735
where the time goes:
time: 135 us; the launch traced here: 134 us
  Pallas kernels  133 us (99%)
    pallas_call x1, Pallas kernels, body(): comm(functools.partial(return_kernel, halves, pieces), 2, (shape(arrived_...  40.9 us
    pallas_call x1, Pallas kernels, body(): comm(functools.partial(spread_kernel, halves), 1, shape(arrived_shape, bf...  33.6 us
    pallas_call x2, Pallas kernels, edges(): pl.pallas_call(functools.partial(edge_kernel, by_slot, n_out), out_shape=...  21.5 us
    pallas_call x1, Pallas kernels, body(): comm(functools.partial(gather_kernel, halves, pieces), 0, (shape((n_rep,...  13.6 us
    pallas_call x1, Pallas kernels, body(): comm(functools.partial(fold_kernel, halves), 3, (shape((rows_dev, width),...  12.9 us
    pallas_call x1, Pallas kernels, body(): pl.pallas_call(node_kernel, out_shape=(shape((rows_dev, width), bf16), sh...  7.99 us

commit v1 on v0

--- a/solution.py
+++ b/solution.py
@@ -692,7 +692,7 @@
         [SMEM, VMEM, VMEM],
         [
             block(n_rep, own_blocks),
-            block(NEIGH, per_rep - per_rep // 2),
+            block(NEIGH, per_rep),
             block(NEIGH, halves, max(per_rep // 2, 1)),
             pltpu.VMEM((halves, n_slab, each, width), bf16),
             many,

time: 135 us -> 130 us (0.963); the launches traced: 134 us -> 131 us
  Pallas kernels: 133 us -> 129 us
    pallas_call x2, Pallas kernels: 21.5 us -> 9.01 us  [edges(): pl.pallas_call(functools.partial(edge_kernel, by_slot, n_out), out_shape=...]
    pallas_call x1, Pallas kernels: 12.9 us -> 19.7 us  [body(): comm(functools.partial(fold_kernel, halves), 3, (shape((rows_dev, width),...]
    pallas_call x1, Pallas kernels: 33.6 us -> 40 us  [body(): comm(functools.partial(spread_kernel, halves), 1, shape(arrived_shape, bf...]
    pallas_call x1, Pallas kernels: 40.9 us -> 36.7 us  [body(): comm(functools.partial(return_kernel, halves, pieces), 2, (shape(arrived_...]
where the time goes in v1:
time: 130 us; the launch traced here: 131 us
  Pallas kernels  129 us (99%)
  between operations  1.31 us (1%)
    pallas_call x1, Pallas kernels, body(): comm(functools.partial(spread_kernel, halves), 1, shape(arrived_shape, bf...  40 us
    pallas_call x1, Pallas kernels, body(): comm(functools.partial(return_kernel, halves, pieces), 2, (shape(arrived_...  36.7 us
    pallas_call x1, Pallas kernels, body(): comm(functools.partial(fold_kernel, halves), 3, (shape((rows_dev, width),...  19.7 us
    pallas_call x1, Pallas kernels, body(): comm(functools.partial(gather_kernel, halves, pieces), 0, (shape((n_rep,...  13.6 us
    pallas_call x2, Pallas kernels, edges(): pl.pallas_call(functools.partial(edge_kernel, by_slot, n_out), out_shape=...  9.01 us
    pallas_call x1, Pallas kernels, body(): pl.pallas_call(node_kernel, out_shape=(shape((rows_dev, width), bf16), sh...  7.93 us

profile of v1, /device:TPU:0, one launch (start us, length us, event | category | flops | bytes accessed | tf_op | source)
XLA Modules:
  0.0 130.8 jit_solution(12464626429798708296)
XLA Ops:
  1.3 13.6 %shard_map.163 = (bf16[4,8,128,128]{3,2,1,0:T(8,128)(2,1)}, bf16[64,128,128]{2,1,0:T(8,128)(2,1)}) custom-call(bf16[8,128,128]{2,1,0:T(8,128)(2,1)} %bitcast.17, bf16[64,128,128]{2,1,0:T(8,128)(2,1)} %table.1), custom_call_target="tpu_custom_call" | custom-call | tf_op jit(solution)/shard_map/pallas_call | solution.py:627
  14.9 4.6 %shard_map.164 = bf16[64,128,128]{2,1,0:T(8,128)(2,1)} custom-call(s32[1]{0:T(128)S(6)} %copy.18.count, s32[1,256]{1,0:T(1,128)} %srcs.3, s32[1,256]{1,0:T(1,128)} %tiles.3, s32[1,256]{1,0:T(1,128)} %slots.3, bf16[64,128,128]{2,1,0:T(8,128)(2,1)} %table.1, bf16[32,128,128]{2,1,0:T(8,128)(2,1)} %bitcast.18), custom_call_target="tpu_custom_call" | custom-call | tf_op jit(solution)/shard_map/pallas_call | solution.py:141
  19.5 40.0 %shard_map.165 = bf16[8,2,2,2,128,128]{5,4,3,2,1,0:T(8,128)(2,1)} custom-call(bf16[8,2,2,2,128,128]{5,4,3,2,1,0:T(8,128)(2,1)} %bitcast.14), custom_call_target="tpu_custom_call" | custom-call | tf_op jit(solution)/shard_map/pallas_call | solution.py:641
  59.5 7.9 %shard_map.166 = (bf16[1024,128]{1,0:T(8,128)(2,1)}, f32[1024,128]{1,0:T(8,128)}, bf16[1024,128]{1,0:T(8,128)(2,1)}, bf16[2048,128]{1,0:T(8,128)(2,1)}) custom-call(s32[8,64]{1,0:T(8,128)} %slot_block.3, bf16[64,128,128]{2,1,0:T(8,128)(2,1)} %bitcast.13, bf16[1024,128]{1,0:T(8,128)(2,1)} %feats.1, bf16[1024,128]{1,0:T(8,128)(2,1)} %cot.1, ...), custom_call_target="tpu_custom_call" | custom-call | tf_op jit(solution)/shard_map/pallas_call | solution.py:659
  67.4 36.7 %shard_map.167 = (bf16[8,2,2,2,128,128]{5,4,3,2,1,0:T(8,128)(2,1)}, bf16[8,64,128]{2,1,0:T(8,128)(2,1)}) custom-call(s32[8,64]{1,0:T(8,128)} %slot_block.3, bf16[8,128,128]{2,1,0:T(8,128)(2,1)} %bitcast.21, bf16[2,2,8,64,128]{4,3,2,1,0:T(8,128)(2,1)} %bitcast.20), custom_call_target="tpu_custom_call" | custom-call | tf_op jit(solution)/shard_map/pallas_call | solution.py:688
  104.1 4.4 %shard_map.168 = bf16[32,128,128]{2,1,0:T(8,128)(2,1)} custom-call(s32[1]{0:T(128)S(6)} %copy.18.count, s32[1,256]{1,0:T(1,128)} %srcs.3, s32[1,256]{1,0:T(1,128)} %tiles.3, s32[1,256]{1,0:T(1,128)} %slots.3, bf16[64,128,128]{2,1,0:T(8,128)(2,1)} %get-tuple-element.24.table, bf16[64,128,128]{2,1,0:T(8,128)(2,1)} %bitcast.16), custom_call_target="tpu_custom_call" | custom-call | tf_op jit(solution)/shard_map/pallas_call | solution.py:141
  108.5 19.7 %shard_map.169 = (f32[1024,128]{1,0:T(8,128)}, bf16[4,8,64,128]{3,2,1,0:T(8,128)(2,1)}) custom-call(bf16[2,2,1024,128]{3,2,1,0:T(8,128)(2,1)} %bitcast.15, bf16[8,64,128]{2,1,0:T(8,128)(2,1)} %get-tuple-element.28.summed), custom_call_target="tpu_custom_call" | custom-call | tf_op jit(solution)/shard_map/pallas_call | solution.py:720
  128.2 2.5 %shard_map.170 = (f32[1024,128]{1,0:T(8,128)}, f32[1,256]{1,0:T(1,128)}, f32[256,512]{1,0:T(8,128)}, f32[1,512]{1,0:T(1,128)}, f32[512,128]{1,0:T(8,128)}) custom-call(f32[1024,128]{1,0:T(8,128)} %get-tuple-element.23.base, f32[1024,128]{1,0:T(8,128)} %get-tuple-element.29.folded, bf16[2048,128]{1,0:T(8,128)(2,1)} %bitcast.19), custom_call_target="tpu_custom_call" | custom-call | tf_op jit(solution)/shard_map/pallas_call | solution.py:735
